TPU v7x, 32 devices: a whole 2x2x4 slice. The times are simulated.
32 devices in a mesh: dp: 4 (over y, x), seq: 8 (over z, core).
Axes of the slice: x: 2, y: 2, z: 4, core: 2. Of those that a mesh axis runs over, the one named last changes fastest.
Arguments:
- tokens: float32 [4, 1024, 1024], P('dp', 'seq'), may hold values from -6 to 6
- cotangent: float32 [4, 1024, 1024], P('dp', 'seq'), may hold values from -6 to 6
- doc_ids: int32 [4, 1024], P('dp'), may hold values from 0 to 1, never falling along the last dimension, each value on 1 to 768 neighbouring positions
- in_weight: float32 [1024, 4384], P(('dp', 'seq')), may hold values from -0.1875 to 0.1875
- out_weight: float32 [1024, 2048], P(('dp', 'seq')), may hold values from -0.125 to 0.125
- in_m: float32 [1024, 4384], P(('dp', 'seq')), may hold values from -30 to 30
- in_v: float32 [1024, 4384], P(('dp', 'seq')), may hold values from 1 to 1000
- out_m: float32 [1024, 2048], P(('dp', 'seq')), may hold values from -30 to 30
- out_v: float32 [1024, 2048], P(('dp', 'seq')), may hold values from 1 to 1000
- vec_params: float32 [14688], replicated, as said below
- vec_m: float32 [14688], replicated, may hold values from -30 to 30
- vec_v: float32 [14688], replicated, may hold values from 1 to 1000
Outputs:
- activations: float32 [4, 1024, 1024], P('dp', 'seq')
- input_grad: float32 [4, 1024, 1024], P('dp', 'seq')
- in_grad: float32 [1024, 4384], P(('dp', 'seq'))
- out_grad: float32 [1024, 2048], P(('dp', 'seq'))
- vec_grad: float32 [14688], replicated
- in_new: float32 [1024, 4384], P(('dp', 'seq'))
- out_new: float32 [1024, 2048], P(('dp', 'seq'))
- vec_new: float32 [14688], replicated
- in_m_new: float32 [1024, 4384], P(('dp', 'seq'))
- in_v_new: float32 [1024, 4384], P(('dp', 'seq'))
- out_m_new: float32 [1024, 2048], P(('dp', 'seq'))
- out_v_new: float32 [1024, 2048], P(('dp', 'seq'))
- vec_m_new: float32 [14688], replicated
- vec_v_new: float32 [14688], replicated
Inputs may be any that keep to these rules, and one draw needn't show every extreme that they name: `doc_ids`: each row holds document 0 and then document 1, each of one or more positions, none longer than 768. `vec_params`: norm_gain and gate_gain lie in 0.7 to 1.3, skip_gain in 0.5 to 1.5, step_bias in -1 to 1, log_rate in -12 to -3.
All inputs are finite; a program needn't handle non-finite values.
Results may differ from a plain program's by a relative error of at most 0.015.
Values may be sent and summed in bfloat16 or wider, within the bound.
A program may use at most 192 MiB of HBM per device.

v0:
```python
import jax
import jax.numpy as jnp
from jax import lax
from jax.sharding import PartitionSpec as P

D = 1024
DI = 2048
H = 32
P_SIZE = 64
N = 128
KW = 4
STRETCH = 256
STEP = 10
CONV = 2304
norm_eps = 1e-05
beta_one = 0.9
beta_two = 0.95
learn_rate = 0.03
decay_rate = 0.1
adam_eps = 1e-08
top_precision = lax.Precision.HIGHEST


def shifted_2(block, axis, distance):
    devices = range(lax.axis_size(axis))
    route = [(i - distance, i) for i in devices if i - distance in devices]
    return lax.ppermute(block, axis, route)


def unpack(vector):
    cursor = D + DI
    norm_gain = vector[:D]
    gate_gain = vector[D:cursor]
    conv_kernel = vector[cursor : cursor + KW * CONV].reshape(KW, CONV)
    cursor = cursor + KW * CONV
    conv_bias = vector[cursor : cursor + CONV]
    cursor = cursor + CONV
    step_bias = vector[cursor : cursor + H]
    log_rate = vector[cursor + H : cursor + 2 * H]
    skip_gain = vector[cursor + 2 * H : cursor + 3 * H]
    return (norm_gain, gate_gain, conv_kernel, conv_bias, step_bias, log_rate, skip_gain)


def repack(norm_gain, gate_gain, conv_kernel, conv_bias, step_bias, log_rate, skip_gain):
    return jnp.concatenate(
        [norm_gain, gate_gain, conv_kernel.reshape(-1), conv_bias, step_bias, log_rate, skip_gain]
    )


def input_norm(inputs, gain):
    scale = lax.rsqrt(jnp.mean(inputs * inputs, axis=-1, keepdims=True) + norm_eps)
    return inputs * scale * gain[None, :]


def gate_norm(ssd_out, gate_in, gain):
    mixed = ssd_out * jax.nn.silu(gate_in)
    scale = lax.rsqrt(jnp.mean(mixed * mixed, axis=-1, keepdims=True) + norm_eps)
    return mixed * scale * gain[None, :]


def conv_silu(padded, conv_kernel, conv_bias, ext_ids):
    length = padded.shape[0] - (KW - 1)
    own_ids = ext_ids[KW - 1 :]
    total = jnp.zeros((length, padded.shape[1]), jnp.float32) + conv_bias[None, :]
    for offset in range(KW):
        valid = (ext_ids[offset : offset + length] == own_ids).astype(jnp.float32)
        total = (
            total + conv_kernel[offset][None, :] * padded[offset : offset + length] * valid[:, None]
        )
    return jax.nn.silu(total)


def rates(step_raw, step_bias, log_rate):
    step_size = jax.nn.softplus(step_raw + step_bias[None, :])
    log_decay = -jnp.exp(log_rate)[None, :] * step_size
    return (step_size, log_decay)


def ssd_block(state, pieces):
    values, input_map, output_map, step_size, log_decay, block_ids, prior_id = pieces
    length = values.shape[0]
    cumulative = jnp.cumsum(log_decay, axis=0)
    rows_index = lax.broadcasted_iota(jnp.int32, (length, length), 0)
    cols_index = lax.broadcasted_iota(jnp.int32, (length, length), 1)
    related = (block_ids[:, None] == block_ids[None, :]) & (rows_index >= cols_index)
    spans = cumulative.T[:, :, None] - cumulative.T[:, None, :]
    decays = jnp.where(related[None], jnp.exp(jnp.where(related[None], spans, 0.0)), 0.0)
    scores = jnp.dot(output_map, input_map.T, precision=top_precision)
    mixing = decays * scores[None] * step_size.T[:, None, :]
    inside = jnp.einsum("hij,jhp->ihp", mixing, values, precision=top_precision)
    carried = (block_ids == prior_id).astype(jnp.float32)
    reach = carried[:, None] * jnp.exp(cumulative)
    entering = (
        jnp.einsum("hpn,in->ihp", state, output_map, precision=top_precision) * reach[:, :, None]
    )
    ending = (block_ids == block_ids[-1]).astype(jnp.float32)
    tail_weight = ending[:, None] * jnp.exp(cumulative[-1][None, :] - cumulative) * step_size
    new_state = state * reach[-1][:, None, None] + jnp.einsum(
        "jh,jhp,jn->hpn", tail_weight, values, input_map, precision=top_precision
    )
    return (new_state, inside + entering)


def ssd_run(mixed_in, step_size, log_decay, skip_gain, row_ids, prior_id, state, block):
    length = mixed_in.shape[0]
    blocks = length // block
    values = mixed_in[:, :DI].reshape(length, H, P_SIZE)
    input_map = mixed_in[:, DI : DI + N]
    output_map = mixed_in[:, DI + N :]
    shifted = jnp.concatenate([jnp.reshape(prior_id, (1,)), row_ids[:-1]])
    priors = shifted.reshape(blocks, block)[:, 0]
    pieces = (
        values.reshape(blocks, block, H, P_SIZE),
        input_map.reshape(blocks, block, N),
        output_map.reshape(blocks, block, N),
        step_size.reshape(blocks, block, H),
        log_decay.reshape(blocks, block, H),
        row_ids.reshape(blocks, block),
        priors,
    )
    final, outputs = lax.scan(ssd_block, state, pieces)
    result = outputs.reshape(length, H, P_SIZE) + skip_gain[None, :, None] * values
    return (result.reshape(length, DI), final)


def adamw_update(param, grad, first, second):
    first_new = beta_one * first + (1.0 - beta_one) * grad
    second_new = beta_two * second + (1.0 - beta_two) * grad * grad
    corrected = first_new / (1.0 - beta_one**STEP)
    scaled = jnp.sqrt(second_new / (1.0 - beta_two**STEP)) + adam_eps
    return (
        param * (1.0 - learn_rate * decay_rate) - learn_rate * corrected / scaled,
        first_new,
        second_new,
    )


def body(
    tokens,
    cotangent,
    doc_ids,
    in_weight,
    out_weight,
    in_m,
    in_v,
    out_m,
    out_v,
    vec_params,
    vec_m,
    vec_v,
):
    in_work, out_work = (
        lax.all_gather(in_weight.astype(jnp.bfloat16), ("dp", "seq"), axis=0, tiled=True),
        lax.all_gather(out_weight.astype(jnp.bfloat16), ("dp", "seq"), axis=0, tiled=True),
    )
    norm_gain, gate_gain, conv_kernel, conv_bias, step_bias, log_rate, skip_gain = unpack(
        vec_params
    )
    inputs = tokens[0]
    upstream_f = cotangent[0]
    local_len = inputs.shape[0]
    block = min(STRETCH, local_len)
    padded_row = jnp.concatenate([jnp.full((KW - 1,), -1, jnp.int32), doc_ids[0]])
    offset = lax.axis_index("seq") * local_len
    ext_ids = lax.dynamic_slice_in_dim(padded_row, offset, local_len + KW - 1)
    own_ids = ext_ids[KW - 1 :]
    prior_id = ext_ids[KW - 2]
    zero_state = jnp.zeros((H, P_SIZE, N), jnp.float32)
    normed = input_norm(inputs, norm_gain).astype(jnp.bfloat16)
    projected = jnp.dot(normed, in_work, preferred_element_type=jnp.float32)
    gate_in = projected[:, :DI]
    conv_in = projected[:, DI : DI + CONV].astype(jnp.bfloat16)
    step_raw = projected[:, DI + CONV :]
    rim = shifted_2(conv_in[local_len - (KW - 1) :], "seq", 1)
    padded = lax.optimization_barrier(jnp.concatenate([rim, conv_in], axis=0)).astype(jnp.float32)
    mixed_in = lax.optimization_barrier(
        conv_silu(padded, conv_kernel, conv_bias, ext_ids).astype(jnp.bfloat16)
    ).astype(jnp.float32)
    output_map = mixed_in[:, DI + N :]

    def pre_chain(mixed, raw, bias_in, rate_in, skip_in):
        step_size, log_decay = rates(raw, bias_in, rate_in)
        local_out, local_state = ssd_run(
            mixed, step_size, log_decay, skip_in, own_ids, prior_id, zero_state, block
        )
        cumulative = jnp.cumsum(log_decay, axis=0)
        reach = (own_ids == prior_id).astype(jnp.float32)[:, None] * jnp.exp(cumulative)
        return (local_out, local_state, reach)

    local_out, local_state, reach = pre_chain(mixed_in, step_raw, step_bias, log_rate, skip_gain)
    decay = reach[-1]

    def relay(turn, entry_now):
        return shifted_2(decay[:, None, None] * entry_now + local_state, "seq", 1)

    entry = lax.fori_loop(0, lax.axis_size("seq") - 1, relay, zero_state)
    entering = (
        jnp.einsum("hpn,tn->thp", entry, output_map, precision=top_precision) * reach[:, :, None]
    )
    ssd_out = local_out + entering.reshape(local_len, DI)
    gated, gate_back = jax.vjp(gate_norm, ssd_out, gate_in, gate_gain)
    normed_out = gated.astype(jnp.bfloat16)
    outputs = inputs + lax.dot_general(
        normed_out, out_work, (((1,), (1,)), ((), ())), preferred_element_type=jnp.float32
    )
    upstream = upstream_f.astype(jnp.bfloat16)
    grad_gated = jnp.dot(upstream, out_work, preferred_element_type=jnp.float32)
    grad_ssd, grad_gate_in, grad_gate_gain = gate_back(grad_gated)
    own_part = jnp.einsum(
        "th,thp,tn->hpn",
        reach,
        grad_ssd.reshape(local_len, H, P_SIZE),
        output_map,
        precision=top_precision,
    )

    def back_relay(turn, later):
        return shifted_2(
            (own_part + decay[:, None, None] * later).astype(jnp.bfloat16), "seq", -1
        ).astype(jnp.float32)

    after = lax.fori_loop(0, lax.axis_size("seq") - 1, back_relay, zero_state)

    def complete(mixed, raw, bias_in, rate_in, skip_in):
        part_out, part_state, part_reach = pre_chain(mixed, raw, bias_in, rate_in, skip_in)
        reader = mixed[:, DI + N :]
        arriving = (
            jnp.einsum("hpn,tn->thp", entry, reader, precision=top_precision)
            * part_reach[:, :, None]
        )
        return (part_out + arriving.reshape(local_len, DI), part_reach[-1], part_state)

    _, ssd_back = jax.vjp(complete, mixed_in, step_raw, step_bias, log_rate, skip_gain)
    grad_mixed, grad_raw, grad_bias, grad_rate, grad_skip = ssd_back(
        (grad_ssd, jnp.sum(after * entry, axis=(1, 2)), after)
    )
    _, conv_back = jax.vjp(
        lambda values, kernel, constant: conv_silu(values, kernel, constant, ext_ids),
        padded,
        conv_kernel,
        conv_bias,
    )
    grad_padded, grad_kernel, grad_cbias = conv_back(grad_mixed)
    returned = shifted_2(grad_padded[: KW - 1], "seq", -1)
    grad_conv = jnp.concatenate(
        [grad_padded[KW - 1 : local_len], grad_padded[local_len:] + returned], axis=0
    )
    grad_proj = jnp.concatenate([grad_gate_in, grad_conv, grad_raw], axis=1).astype(jnp.bfloat16)
    grad_normed = lax.dot_general(
        grad_proj, in_work, (((1,), (1,)), ((), ())), preferred_element_type=jnp.float32
    )
    _, norm_back = jax.vjp(input_norm, inputs, norm_gain)
    grad_inputs, grad_norm_gain = norm_back(grad_normed)
    vector = repack(
        grad_norm_gain, grad_gate_gain, grad_kernel, grad_cbias, grad_bias, grad_rate, grad_skip
    )
    dp_count = lax.axis_size("dp")
    seq_count = lax.axis_size("seq")
    owner_rows = in_weight.shape[0]
    seq_place = lax.axis_index("seq")

    def select_rows(matrix):
        count = matrix.shape[0]
        grouped = matrix.reshape(count, dp_count, seq_count, owner_rows)
        chosen = lax.dynamic_slice_in_dim(grouped, seq_place, 1, 2)
        return chosen.reshape(count, dp_count * owner_rows)

    normed_piece = lax.all_gather(normed, "seq", axis=0, tiled=True)
    proj_piece = lax.all_gather(grad_proj, "seq", axis=0, tiled=True)
    upstream_piece = lax.all_gather(upstream, "seq", axis=0, tiled=True)
    out_piece = lax.all_gather(normed_out, "seq", axis=0, tiled=True)
    first = lax.dot_general(
        select_rows(normed_piece),
        proj_piece,
        (((0,), (0,)), ((), ())),
        preferred_element_type=jnp.float32,
    )
    second = lax.dot_general(
        select_rows(upstream_piece),
        out_piece,
        (((0,), (0,)), ((), ())),
        preferred_element_type=jnp.float32,
    )
    in_part, out_part = (
        lax.psum_scatter(
            first.reshape(dp_count, owner_rows, grad_proj.shape[1]).astype(jnp.bfloat16),
            "dp",
            scatter_dimension=0,
            tiled=True,
        ).astype(jnp.float32),
        lax.psum_scatter(
            second.reshape(dp_count, owner_rows, normed_out.shape[1]).astype(jnp.bfloat16),
            "dp",
            scatter_dimension=0,
            tiled=True,
        ).astype(jnp.float32),
    )
    in_grad = in_part.reshape(owner_rows, grad_proj.shape[1])
    out_grad = out_part.reshape(owner_rows, normed_out.shape[1])
    vec_grad = lax.psum(vector, ("dp", "seq"))
    in_new, in_m_new, in_v_new = adamw_update(in_weight, in_grad, in_m, in_v)
    out_new, out_m_new, out_v_new = adamw_update(out_weight, out_grad, out_m, out_v)
    vec_new, vec_m_new, vec_v_new = adamw_update(vec_params, vec_grad, vec_m, vec_v)
    return (
        outputs[None],
        (upstream_f + grad_inputs)[None],
        in_grad,
        out_grad,
        vec_grad,
        in_new,
        out_new,
        vec_new,
        in_m_new,
        in_v_new,
        out_m_new,
        out_v_new,
        vec_m_new,
        vec_v_new,
    )


def solution(mesh):
    in_specs = (
        P("dp", "seq", None),
        P("dp", "seq", None),
        P("dp", None),
        P(("dp", "seq"), None),
        P(("dp", "seq"), None),
        P(("dp", "seq"), None),
        P(("dp", "seq"), None),
        P(("dp", "seq"), None),
        P(("dp", "seq"), None),
        P(),
        P(),
        P(),
    )
    out_specs = (
        P("dp", "seq", None),
        P("dp", "seq", None),
        P(("dp", "seq"), None),
        P(("dp", "seq"), None),
        P(),
        P(("dp", "seq"), None),
        P(("dp", "seq"), None),
        P(),
        P(("dp", "seq"), None),
        P(("dp", "seq"), None),
        P(("dp", "seq"), None),
        P(("dp", "seq"), None),
        P(),
        P(),
    )
    return jax.shard_map(body, mesh=mesh, in_specs=in_specs, out_specs=out_specs, check_vma=False)
```

profile of v0, /device:TPU:0, one launch (start us, length us, event | category | flops | bytes accessed | tf_op | source)
XLA Modules:
  0.0 678.0 jit_solution(5091734478298455227)
XLA Ops:
  17.9 76.6 %all-gather.7.cloned.1.call-done = bf16[1024,4384]{1,0:T(8,128)(2,1)} async-done(((bf16[32,4384]{1,0:T(8,128)(2,1)}), bf16[1024,4384]{1,0:T(8,128)(2,1)}) %all-gather.7.cloned.1.call-update) | async-done | bytes 8978448 | tf_op jit(solution)/shard_map/all_gather | solution.py:153
  94.5 5.1 fusion.124
  128.1 152.6 %while.7 = (s32[]{:T(128)}, f32[32,64,128]{2,1,0:T(8,128)S(1)}, f32[1,32]{1,0:T(1,128)S(1)}, f32[32,64,128]{2,1,0:T(8,128)}, s32[]{:T(128)}) while((s32[]{:T(128)}, f32[32,64,128]{2,1,0:T(8,128)S(1)}, f32[1,32]{1,0:T(1,128)S(1)}, f32[32,64,128]{2,1,0:T(8,128)}, s32[]{:T(128)}) %tuple.149), condition=%wide.region_3.4_spmd, body=%wide.region_2.3_spmd.sunk | while | flops 524290 | bytes 7340261 | solution.py:196
  138.4 23.1 %collective-permute-start = (f32[32,64,128]{2,1,0:T(8,128)}, f32[32,64,128]{2,1,0:T(8,128)S(1)}, u32[]{:S(2)}, u32[]{:S(2)}) collective-permute-start(f32[32,64,128]{2,1,0:T(8,128)} %multiply_add_fusion.13), channel_id=1, source_target_pairs={{0,1},{1,2},{2,3},{3,4},{4,5},{5,6},{6,7},{8,9},{9,10},{10,11},{11... | collective-permute-start | bytes 3145736 | tf_op jit(solution)/shard_map/while/body/eval_jaxpr/ppermute | solution.py:27
  166.3 27.7 %collective-permute-start = (f32[32,64,128]{2,1,0:T(8,128)}, f32[32,64,128]{2,1,0:T(8,128)S(1)}, u32[]{:S(2)}, u32[]{:S(2)}) collective-permute-start(f32[32,64,128]{2,1,0:T(8,128)} %multiply_add_fusion.13), channel_id=1, source_target_pairs={{0,1},{1,2},{2,3},{3,4},{4,5},{5,6},{6,7},{8,9},{9,10},{10,11},{11... | collective-permute-start | bytes 3145736 | tf_op jit(solution)/shard_map/while/body/eval_jaxpr/ppermute | solution.py:27
  198.8 22.8 %collective-permute-start = (f32[32,64,128]{2,1,0:T(8,128)}, f32[32,64,128]{2,1,0:T(8,128)S(1)}, u32[]{:S(2)}, u32[]{:S(2)}) collective-permute-start(f32[32,64,128]{2,1,0:T(8,128)} %multiply_add_fusion.13), channel_id=1, source_target_pairs={{0,1},{1,2},{2,3},{3,4},{4,5},{5,6},{6,7},{8,9},{9,10},{10,11},{11... | collective-permute-start | bytes 3145736 | tf_op jit(solution)/shard_map/while/body/eval_jaxpr/ppermute | solution.py:27
  226.4 14.3 %collective-permute-start = (f32[32,64,128]{2,1,0:T(8,128)}, f32[32,64,128]{2,1,0:T(8,128)S(1)}, u32[]{:S(2)}, u32[]{:S(2)}) collective-permute-start(f32[32,64,128]{2,1,0:T(8,128)} %multiply_add_fusion.13), channel_id=1, source_target_pairs={{0,1},{1,2},{2,3},{3,4},{4,5},{5,6},{6,7},{8,9},{9,10},{10,11},{11... | collective-permute-start | bytes 3145736 | tf_op jit(solution)/shard_map/while/body/eval_jaxpr/ppermute | solution.py:27
  245.6 13.9 %collective-permute-start = (f32[32,64,128]{2,1,0:T(8,128)}, f32[32,64,128]{2,1,0:T(8,128)S(1)}, u32[]{:S(2)}, u32[]{:S(2)}) collective-permute-start(f32[32,64,128]{2,1,0:T(8,128)} %multiply_add_fusion.13), channel_id=1, source_target_pairs={{0,1},{1,2},{2,3},{3,4},{4,5},{5,6},{6,7},{8,9},{9,10},{10,11},{11... | collective-permute-start | bytes 3145736 | tf_op jit(solution)/shard_map/while/body/eval_jaxpr/ppermute | solution.py:27
  264.3 13.9 %collective-permute-start = (f32[32,64,128]{2,1,0:T(8,128)}, f32[32,64,128]{2,1,0:T(8,128)S(1)}, u32[]{:S(2)}, u32[]{:S(2)}) collective-permute-start(f32[32,64,128]{2,1,0:T(8,128)} %multiply_add_fusion.13), channel_id=1, source_target_pairs={{0,1},{1,2},{2,3},{3,4},{4,5},{5,6},{6,7},{8,9},{9,10},{10,11},{11... | collective-permute-start | bytes 3145736 | tf_op jit(solution)/shard_map/while/body/eval_jaxpr/ppermute | solution.py:27
  308.9 5.2 fusion.35
  323.6 134.3 %while.16 = (s32[]{:T(128)}, f32[32,64,128]{2,1,0:T(8,128)S(1)}, f32[1,32]{1,0:T(1,128)S(1)}, f32[32,64,128]{2,1,0:T(8,128)}, s32[]{:T(128)}, /*index=5*/s32[]{:T(128)}) while((s32[]{:T(128)}, f32[32,64,128]{2,1,0:T(8,128)S(1)}, f32[1,32]{1,0:T(1,128)S(1)}, f32[32,64,128]{2,1,0:T(8,128)}, s32[]{:T(128)}, ...), condition=%wide.region_8.9_spmd.clone, body=%wide.region_7.8_spmd.clone.sunk | while | flops 1310723 | bytes 6291703 | solution.py:222
  327.1 14.3 %collective-permute-done.1 = bf16[32,64,128]{2,1,0:T(8,128)(2,1)} collective-permute-done((bf16[32,64,128]{2,1,0:T(8,128)(2,1)}, bf16[32,64,128]{2,1,0:T(8,128)(2,1)}, u32[]{:S(2)}, u32[]{:S(2)}) %collective-permute-start.1) | collective-permute-done | bytes 524320 | tf_op jit(solution)/shard_map/while/body/eval_jaxpr/ppermute | solution.py:27
  346.0 10.2 %collective-permute-done.1 = bf16[32,64,128]{2,1,0:T(8,128)(2,1)} collective-permute-done((bf16[32,64,128]{2,1,0:T(8,128)(2,1)}, bf16[32,64,128]{2,1,0:T(8,128)(2,1)}, u32[]{:S(2)}, u32[]{:S(2)}) %collective-permute-start.1) | collective-permute-done | bytes 524320 | tf_op jit(solution)/shard_map/while/body/eval_jaxpr/ppermute | solution.py:27
  360.9 39.0 %collective-permute-done.1 = bf16[32,64,128]{2,1,0:T(8,128)(2,1)} collective-permute-done((bf16[32,64,128]{2,1,0:T(8,128)(2,1)}, bf16[32,64,128]{2,1,0:T(8,128)(2,1)}, u32[]{:S(2)}, u32[]{:S(2)}) %collective-permute-start.1) | collective-permute-done | bytes 524320 | tf_op jit(solution)/shard_map/while/body/eval_jaxpr/ppermute | solution.py:27
  404.5 9.5 %collective-permute-done.1 = bf16[32,64,128]{2,1,0:T(8,128)(2,1)} collective-permute-done((bf16[32,64,128]{2,1,0:T(8,128)(2,1)}, bf16[32,64,128]{2,1,0:T(8,128)(2,1)}, u32[]{:S(2)}, u32[]{:S(2)}) %collective-permute-start.1) | collective-permute-done | bytes 524320 | tf_op jit(solution)/shard_map/while/body/eval_jaxpr/ppermute | solution.py:27
  418.7 9.5 %collective-permute-done.1 = bf16[32,64,128]{2,1,0:T(8,128)(2,1)} collective-permute-done((bf16[32,64,128]{2,1,0:T(8,128)(2,1)}, bf16[32,64,128]{2,1,0:T(8,128)(2,1)}, u32[]{:S(2)}, u32[]{:S(2)}) %collective-permute-start.1) | collective-permute-done | bytes 524320 | tf_op jit(solution)/shard_map/while/body/eval_jaxpr/ppermute | solution.py:27
  432.8 9.5 %collective-permute-done.1 = bf16[32,64,128]{2,1,0:T(8,128)(2,1)} collective-permute-done((bf16[32,64,128]{2,1,0:T(8,128)(2,1)}, bf16[32,64,128]{2,1,0:T(8,128)(2,1)}, u32[]{:S(2)}, u32[]{:S(2)}) %collective-permute-start.1) | collective-permute-done | bytes 524320 | tf_op jit(solution)/shard_map/while/body/eval_jaxpr/ppermute | solution.py:27
  447.0 9.5 %collective-permute-done.1 = bf16[32,64,128]{2,1,0:T(8,128)(2,1)} collective-permute-done((bf16[32,64,128]{2,1,0:T(8,128)(2,1)}, bf16[32,64,128]{2,1,0:T(8,128)(2,1)}, u32[]{:S(2)}, u32[]{:S(2)}) %collective-permute-start.1) | collective-permute-done | bytes 524320 | tf_op jit(solution)/shard_map/while/body/eval_jaxpr/ppermute | solution.py:27
  476.2 5.1 fusion.28
  505.8 7.9 %collective-permute-done.3 = f32[3,2304]{1,0:T(4,128)S(1)} collective-permute-done((f32[3,2304]{1,0:T(4,128)S(1)}, f32[3,2304]{1,0:T(4,128)S(1)}, u32[]{:S(2)}, u32[]{:S(2)}) %collective-permute-start.3) | collective-permute-done | bytes 27680 | tf_op jit(solution)/shard_map/ppermute | solution.py:27
  530.9 78.9 %all-gather.13.cloned.1.call-done = bf16[1024,4384]{1,0:T(8,128)(2,1)} async-done(((bf16[128,4384]{1,0:T(8,128)(2,1)}), bf16[1024,4384]{1,0:T(8,128)(2,1)}) %all-gather.13.cloned.1.call-update) | async-done | bytes 8978448 | tf_op jit(solution)/shard_map/all_gather | solution.py:269
  609.9 6.0 fusion.4
  617.2 7.0 %multiply_reduce_fusion.14 = (f32[1024]{0:T(1024)S(1)}, f32[128]{0:T(128)S(1)}, f32[128,1024]{1,0:T(8,128)S(1)}) fusion(f32[1,128,1024]{2,1,0:T(8,128)S(1)} %copy-done.2, f32[128]{0:T(128)S(1)} %copy-done.78, f32[1024]{0:T(1024)S(1)} %slice.169, bf16[128,4384]{1,0:T(8,128)(2,1)S(1)} %copy-done.3, bf16[1024,4384]{1,0:T(8,128)(2,1)} %all-gather.7.cloned.1.call-done), kind=kOutput, calls=%fused_computation.102 | convolution fusion | flops 1150024576 | bytes 11158528 | tf_op jit(solution)/shard_map/dot_general | solution.py:249
  624.3 39.2 %psum.7 = f32[14688]{0:T(1024)S(1)} all-reduce(f32[14688]{0:T(1024)S(1)} %concatenate.23), channel_id=1, replica_groups=mesh['dp'=4,'seq'=8] {'dp','seq'}, use_global_device_ids=true, to_apply=%region_33.34 | all-reduce | flops 14688 | bytes 117504 | tf_op jit(solution)/shard_map/psum | solution.py:300
  (333 shorter events, 213.5 us)
Async XLA Ops:
  7.2 87.3 %all-gather.7.cloned.1.call-start = ((), (), s32[]{:S(2)}) async-start(), calls=%async_computation.2 | async-start | bytes 9461760 | tf_op jit(solution)/shard_map/all_gather | solution.py:153
  9.1 288.6 %all-gather.9.cloned.1.call-start = ((), (), s32[]{:S(2)}) async-start(), calls=%async_computation.3 | async-start | bytes 4325376 | tf_op jit(solution)/shard_map/all_gather | solution.py:154
  9.9 505.0 %all-gather.11.cloned.1.call-start = ((), (), s32[]{:S(2)}) async-start(), calls=%async_computation.4 | async-start | bytes 2359296 | tf_op jit(solution)/shard_map/all_gather | solution.py:268
  11.0 506.9 %all-gather.15.cloned.1.call-start = ((), (), s32[]{:S(2)}) async-start(), calls=%async_computation.6 | async-start | bytes 2359296 | tf_op jit(solution)/shard_map/all_gather | solution.py:270
  11.8 510.1 %all-gather.17.cloned.1.call-start = ((), (), s32[]{:S(2)}) async-start(), calls=%async_computation.7 | async-start | bytes 4718592 | tf_op jit(solution)/shard_map/all_gather | solution.py:271
  101.3 16.9 %collective-permute-start.2 = (bf16[3,2304]{1,0:T(4,128)(2,1)}, bf16[3,2304]{1,0:T(4,128)(2,1)}, u32[]{:S(2)}, u32[]{:S(2)}) collective-permute-start(bf16[3,2304]{1,0:T(4,128)(2,1)} %slice.205), channel_id=1, source_target_pairs={{0,1},{1,2},{2,3},{3,4},{4,5},{5,6},{6,7},{8,9},{9,10},{10,11},{11... | collective-permute-start | bytes 41480 | tf_op jit(solution)/shard_map/ppermute | solution.py:27
  130.9 5.0 collective-permute-start
  138.4 25.5 %collective-permute-start = (f32[32,64,128]{2,1,0:T(8,128)}, f32[32,64,128]{2,1,0:T(8,128)S(1)}, u32[]{:S(2)}, u32[]{:S(2)}) collective-permute-start(f32[32,64,128]{2,1,0:T(8,128)} %multiply_add_fusion.13), channel_id=1, source_target_pairs={{0,1},{1,2},{2,3},{3,4},{4,5},{5,6},{6,7},{8,9},{9,10},{10,11},{11... | collective-permute-start | bytes 3145736 | tf_op jit(solution)/shard_map/while/body/eval_jaxpr/ppermute | solution.py:27
  166.3 30.1 %collective-permute-start = (f32[32,64,128]{2,1,0:T(8,128)}, f32[32,64,128]{2,1,0:T(8,128)S(1)}, u32[]{:S(2)}, u32[]{:S(2)}) collective-permute-start(f32[32,64,128]{2,1,0:T(8,128)} %multiply_add_fusion.13), channel_id=1, source_target_pairs={{0,1},{1,2},{2,3},{3,4},{4,5},{5,6},{6,7},{8,9},{9,10},{10,11},{11... | collective-permute-start | bytes 3145736 | tf_op jit(solution)/shard_map/while/body/eval_jaxpr/ppermute | solution.py:27
  198.8 25.3 %collective-permute-start = (f32[32,64,128]{2,1,0:T(8,128)}, f32[32,64,128]{2,1,0:T(8,128)S(1)}, u32[]{:S(2)}, u32[]{:S(2)}) collective-permute-start(f32[32,64,128]{2,1,0:T(8,128)} %multiply_add_fusion.13), channel_id=1, source_target_pairs={{0,1},{1,2},{2,3},{3,4},{4,5},{5,6},{6,7},{8,9},{9,10},{10,11},{11... | collective-permute-start | bytes 3145736 | tf_op jit(solution)/shard_map/while/body/eval_jaxpr/ppermute | solution.py:27
  226.4 16.7 %collective-permute-start = (f32[32,64,128]{2,1,0:T(8,128)}, f32[32,64,128]{2,1,0:T(8,128)S(1)}, u32[]{:S(2)}, u32[]{:S(2)}) collective-permute-start(f32[32,64,128]{2,1,0:T(8,128)} %multiply_add_fusion.13), channel_id=1, source_target_pairs={{0,1},{1,2},{2,3},{3,4},{4,5},{5,6},{6,7},{8,9},{9,10},{10,11},{11... | collective-permute-start | bytes 3145736 | tf_op jit(solution)/shard_map/while/body/eval_jaxpr/ppermute | solution.py:27
  245.6 16.3 %collective-permute-start = (f32[32,64,128]{2,1,0:T(8,128)}, f32[32,64,128]{2,1,0:T(8,128)S(1)}, u32[]{:S(2)}, u32[]{:S(2)}) collective-permute-start(f32[32,64,128]{2,1,0:T(8,128)} %multiply_add_fusion.13), channel_id=1, source_target_pairs={{0,1},{1,2},{2,3},{3,4},{4,5},{5,6},{6,7},{8,9},{9,10},{10,11},{11... | collective-permute-start | bytes 3145736 | tf_op jit(solution)/shard_map/while/body/eval_jaxpr/ppermute | solution.py:27
  264.3 16.3 %collective-permute-start = (f32[32,64,128]{2,1,0:T(8,128)}, f32[32,64,128]{2,1,0:T(8,128)S(1)}, u32[]{:S(2)}, u32[]{:S(2)}) collective-permute-start(f32[32,64,128]{2,1,0:T(8,128)} %multiply_add_fusion.13), channel_id=1, source_target_pairs={{0,1},{1,2},{2,3},{3,4},{4,5},{5,6},{6,7},{8,9},{9,10},{10,11},{11... | collective-permute-start | bytes 3145736 | tf_op jit(solution)/shard_map/while/body/eval_jaxpr/ppermute | solution.py:27
  323.5 286.4 %all-gather.13.cloned.1.call-start = ((), (), s32[]{:S(2)}) async-start(), calls=%async_computation.5 | async-start | bytes 10321920 | tf_op jit(solution)/shard_map/all_gather | solution.py:269
  325.8 15.6 %collective-permute-start.1 = (bf16[32,64,128]{2,1,0:T(8,128)(2,1)}, bf16[32,64,128]{2,1,0:T(8,128)(2,1)}, u32[]{:S(2)}, u32[]{:S(2)}) collective-permute-start(bf16[32,64,128]{2,1,0:T(8,128)(2,1)} %fusion.145), channel_id=1, source_target_pairs={{1,0},{2,1},{3,2},{4,3},{5,4},{6,5},{7,6},{9,8},{10,9},{11,10},{12... | collective-permute-start | bytes 1572872 | tf_op jit(solution)/shard_map/while/body/eval_jaxpr/ppermute | solution.py:27
  344.7 11.4 %collective-permute-start.1 = (bf16[32,64,128]{2,1,0:T(8,128)(2,1)}, bf16[32,64,128]{2,1,0:T(8,128)(2,1)}, u32[]{:S(2)}, u32[]{:S(2)}) collective-permute-start(bf16[32,64,128]{2,1,0:T(8,128)(2,1)} %fusion.145), channel_id=1, source_target_pairs={{1,0},{2,1},{3,2},{4,3},{5,4},{6,5},{7,6},{9,8},{10,9},{11,10},{12... | collective-permute-start | bytes 1572872 | tf_op jit(solution)/shard_map/while/body/eval_jaxpr/ppermute | solution.py:27
  359.6 40.2 %collective-permute-start.1 = (bf16[32,64,128]{2,1,0:T(8,128)(2,1)}, bf16[32,64,128]{2,1,0:T(8,128)(2,1)}, u32[]{:S(2)}, u32[]{:S(2)}) collective-permute-start(bf16[32,64,128]{2,1,0:T(8,128)(2,1)} %fusion.145), channel_id=1, source_target_pairs={{1,0},{2,1},{3,2},{4,3},{5,4},{6,5},{7,6},{9,8},{10,9},{11,10},{12... | collective-permute-start | bytes 1572872 | tf_op jit(solution)/shard_map/while/body/eval_jaxpr/ppermute | solution.py:27
  403.2 10.8 %collective-permute-start.1 = (bf16[32,64,128]{2,1,0:T(8,128)(2,1)}, bf16[32,64,128]{2,1,0:T(8,128)(2,1)}, u32[]{:S(2)}, u32[]{:S(2)}) collective-permute-start(bf16[32,64,128]{2,1,0:T(8,128)(2,1)} %fusion.145), channel_id=1, source_target_pairs={{1,0},{2,1},{3,2},{4,3},{5,4},{6,5},{7,6},{9,8},{10,9},{11,10},{12... | collective-permute-start | bytes 1572872 | tf_op jit(solution)/shard_map/while/body/eval_jaxpr/ppermute | solution.py:27
  417.4 10.8 %collective-permute-start.1 = (bf16[32,64,128]{2,1,0:T(8,128)(2,1)}, bf16[32,64,128]{2,1,0:T(8,128)(2,1)}, u32[]{:S(2)}, u32[]{:S(2)}) collective-permute-start(bf16[32,64,128]{2,1,0:T(8,128)(2,1)} %fusion.145), channel_id=1, source_target_pairs={{1,0},{2,1},{3,2},{4,3},{5,4},{6,5},{7,6},{9,8},{10,9},{11,10},{12... | collective-permute-start | bytes 1572872 | tf_op jit(solution)/shard_map/while/body/eval_jaxpr/ppermute | solution.py:27
  431.6 10.8 %collective-permute-start.1 = (bf16[32,64,128]{2,1,0:T(8,128)(2,1)}, bf16[32,64,128]{2,1,0:T(8,128)(2,1)}, u32[]{:S(2)}, u32[]{:S(2)}) collective-permute-start(bf16[32,64,128]{2,1,0:T(8,128)(2,1)} %fusion.145), channel_id=1, source_target_pairs={{1,0},{2,1},{3,2},{4,3},{5,4},{6,5},{7,6},{9,8},{10,9},{11,10},{12... | collective-permute-start | bytes 1572872 | tf_op jit(solution)/shard_map/while/body/eval_jaxpr/ppermute | solution.py:27
  445.7 10.8 %collective-permute-start.1 = (bf16[32,64,128]{2,1,0:T(8,128)(2,1)}, bf16[32,64,128]{2,1,0:T(8,128)(2,1)}, u32[]{:S(2)}, u32[]{:S(2)}) collective-permute-start(bf16[32,64,128]{2,1,0:T(8,128)(2,1)} %fusion.145), channel_id=1, source_target_pairs={{1,0},{2,1},{3,2},{4,3},{5,4},{6,5},{7,6},{9,8},{10,9},{11,10},{12... | collective-permute-start | bytes 1572872 | tf_op jit(solution)/shard_map/while/body/eval_jaxpr/ppermute | solution.py:27
  503.9 9.8 %collective-permute-start.3 = (f32[3,2304]{1,0:T(4,128)S(1)}, f32[3,2304]{1,0:T(4,128)S(1)}, u32[]{:S(2)}, u32[]{:S(2)}) collective-permute-start(f32[3,2304]{1,0:T(4,128)S(1)} %pad_add_fusion.1), channel_id=1, source_target_pairs={{1,0},{2,1},{3,2},{4,3},{5,4},{6,5},{7,6},{9,8},{10,9},{11,10},{12... | collective-permute-start | bytes 82952 | tf_op jit(solution)/shard_map/ppermute | solution.py:27
  514.9 151.3 %reduce-scatter.9.cloned.1.call-start = ((), (), s32[]{:S(2)}) async-start(), calls=%async_computation.9 | async-start | bytes 655360
  525.9 142.6 %reduce-scatter.7.cloned.1.call-start = ((), (), s32[]{:S(2)}) async-start(), calls=%async_computation.8 | async-start | bytes 1433600
  (84 other events, 852.3 us)
Sparse Core Ops, SparseCore 0:
  11.4 82.9 all-gather.6
  98.1 60.2 all-gather.8
  160.5 32.0 all-gather.10
  194.6 31.4 all-gather.14
  323.6 73.2 all-gather.16
  515.0 94.8 all-gather.12
  613.3 23.5 reduce-scatter.8
  639.7 28.6 reduce-scatter.6
where the time goes:
time: 686 us; the launch traced here: 678 us
  waiting for transfers between devices  282 us (41%)
  starting transfers between devices  132 us (19%)
  other arithmetic  89.3 us (13%)
  matrix products  67.5 us (10%)
  local copies, waits for them, and re-layouts  51.8 us (8%)
  blocking collectives  39.2 us (6%)
  between operations  15.4 us (2%)
    ppermute x16, starting transfers between devices, shifted_2(): return lax.ppermute(block, axis, route)  131 us
    ppermute x16, waiting for transfers between devices, shifted_2(): return lax.ppermute(block, axis, route)  126 us
    all_gather x1, waiting for transfers between devices, body(): proj_piece = lax.all_gather(grad_proj, 'seq', axis=0, tiled=True)  78.9 us
    all_gather x1, waiting for transfers between devices, body(): lax.all_gather(in_weight.astype(jnp.bfloat16), ('dp', 'seq'), axis=0, til...  76.6 us
    psum x1, blocking collectives, body(): vec_grad = lax.psum(vector, ('dp', 'seq'))  39.2 us
    add x7, other arithmetic, relay(): return shifted_2(decay[:, None, None] * entry_now + local_state, 'seq', 1)  16.8 us
    convert_element_type x7, other arithmetic, back_relay(): (own_part + decay[:, None, None] * later).astype(jnp.bfloat16)  15.5 us
    dot_general x3, matrix products, ssd_block(): inside = jnp.einsum('hij,jhp->ihp', mixing, values, precision=top_precision)  13.7 us
  transfers between devices with their start and end apart: 24, of which 18 were waited for; matrix products, arithmetic and copies ran while one was open for 30% of the time, Pallas kernels for 0%

commit v1 on v0

--- a/solution.py
+++ b/solution.py
@@ -149,6 +149,11 @@
     vec_m,
     vec_v,
 ):
+
+    def divide_slices_up(original):
+        val2 = jax.lax.all_gather(original, ("dp", "seq")).sum(axis=0)
+        return val2
+
     in_work, out_work = (
         lax.all_gather(in_weight.astype(jnp.bfloat16), ("dp", "seq"), axis=0, tiled=True),
         lax.all_gather(out_weight.astype(jnp.bfloat16), ("dp", "seq"), axis=0, tiled=True),
@@ -297,7 +302,7 @@
     )
     in_grad = in_part.reshape(owner_rows, grad_proj.shape[1])
     out_grad = out_part.reshape(owner_rows, normed_out.shape[1])
-    vec_grad = lax.psum(vector, ("dp", "seq"))
+    vec_grad = divide_slices_up(vector)
     in_new, in_m_new, in_v_new = adamw_update(in_weight, in_grad, in_m, in_v)
     out_new, out_m_new, out_v_new = adamw_update(out_weight, out_grad, out_m, out_v)
     vec_new, vec_m_new, vec_v_new = adamw_update(vec_params, vec_grad, vec_m, vec_v)

time: 686 us -> 801 us (1.17)
  waiting for transfers between devices: 282 us -> 448 us
  blocking collectives: 39.2 us -> 0 us
  other arithmetic: 89.3 us -> 76.3 us
    unnamed x10 -> x12, waiting for transfers between devices: 0.41 us -> 179 us
    psum x1 -> x0, blocking collectives: 39.2 us -> none  [body(): vec_grad = lax.psum(vector, ('dp', 'seq'))]
    all_gather x1, starting transfers between devices: 0.04 us -> 12.5 us  [body(): proj_piece = lax.all_gather(grad_proj, 'seq', axis=0, tiled=True)]
    add x7, other arithmetic: 16.8 us -> 8.22 us  [relay(): return shifted_2(decay[:, None, None] * entry_now + local_state, 'seq', 1)]
    all_gather x1, waiting for transfers between devices: 78.9 us -> 70.4 us  [body(): proj_piece = lax.all_gather(grad_proj, 'seq', axis=0, tiled=True)]
  transfers between devices with their start and end apart: 24 -> 25, of which waited for: 18 -> 20; matrix products, arithmetic and copies ran while one was open for 30% -> 22% of each run, Pallas kernels for 0% -> 0%
where the time goes in v1:
time: 801 us; the launch traced here: 791 us
  waiting for transfers between devices  448 us (56%)
  starting transfers between devices  140 us (17%)
  other arithmetic  76.3 us (10%)
  matrix products  64.5 us (8%)
  local copies, waits for them, and re-layouts  45.9 us (6%)
  between operations  15.3 us (2%)
    unnamed x12, waiting for transfers between devices  179 us
    ppermute x16, starting transfers between devices, shifted_2(): return lax.ppermute(block, axis, route)  127 us
    ppermute x16, waiting for transfers between devices, shifted_2(): return lax.ppermute(block, axis, route)  121 us
    all_gather x1, waiting for transfers between devices, body(): lax.all_gather(in_weight.astype(jnp.bfloat16), ('dp', 'seq'), axis=0, til...  78 us
    all_gather x1, waiting for transfers between devices, body(): proj_piece = lax.all_gather(grad_proj, 'seq', axis=0, tiled=True)  70.4 us
  transfers between devices with their start and end apart: 25, of which 20 were waited for; matrix products, arithmetic and copies ran while one was open for 22% of the time, Pallas kernels for 0%

profile of v1, /device:TPU:0, one launch (start us, length us, event | category | flops | bytes accessed | tf_op | source)
XLA Modules:
  0.0 791.0 jit_solution(7889474800737952014)
XLA Ops:
  16.6 78.0 %all-gather.8.cloned.1.call-done = bf16[1024,4384]{1,0:T(8,128)(2,1)} async-done(((bf16[32,4384]{1,0:T(8,128)(2,1)}), bf16[1024,4384]{1,0:T(8,128)(2,1)}) %all-gather.8.cloned.1.call-update) | async-done | bytes 8978448 | tf_op jit(solution)/shard_map/all_gather | solution.py:158
  114.4 140.7 %while.7 = (s32[]{:T(128)}, f32[32,64,128]{2,1,0:T(8,128)S(1)}, f32[1,32]{1,0:T(1,128)S(1)}, f32[32,64,128]{2,1,0:T(8,128)S(1)}, s32[]{:T(128)}) while((s32[]{:T(128)}, f32[32,64,128]{2,1,0:T(8,128)S(1)}, f32[1,32]{1,0:T(1,128)S(1)}, f32[32,64,128]{2,1,0:T(8,128)S(1)}, s32[]{:T(128)}) %tuple.151), condition=%wide.region_3.4_spmd, body=%wide.region_2.3_spmd.sunk | while | flops 524290 | bytes 7340261 | solution.py:201
  122.4 17.4 %collective-permute-start = (f32[32,64,128]{2,1,0:T(8,128)}, f32[32,64,128]{2,1,0:T(8,128)S(1)}, u32[]{:S(2)}, u32[]{:S(2)}) collective-permute-start(f32[32,64,128]{2,1,0:T(8,128)} %multiply_add_fusion.13), channel_id=1, source_target_pairs={{0,1},{1,2},{2,3},{3,4},{4,5},{5,6},{6,7},{8,9},{9,10},{10,11},{11... | collective-permute-start | bytes 3145736 | tf_op jit(solution)/shard_map/while/body/eval_jaxpr/ppermute | solution.py:27
  144.0 21.9 %collective-permute-start = (f32[32,64,128]{2,1,0:T(8,128)}, f32[32,64,128]{2,1,0:T(8,128)S(1)}, u32[]{:S(2)}, u32[]{:S(2)}) collective-permute-start(f32[32,64,128]{2,1,0:T(8,128)} %multiply_add_fusion.13), channel_id=1, source_target_pairs={{0,1},{1,2},{2,3},{3,4},{4,5},{5,6},{6,7},{8,9},{9,10},{10,11},{11... | collective-permute-start | bytes 3145736 | tf_op jit(solution)/shard_map/while/body/eval_jaxpr/ppermute | solution.py:27
  169.5 30.7 %collective-permute-start = (f32[32,64,128]{2,1,0:T(8,128)}, f32[32,64,128]{2,1,0:T(8,128)S(1)}, u32[]{:S(2)}, u32[]{:S(2)}) collective-permute-start(f32[32,64,128]{2,1,0:T(8,128)} %multiply_add_fusion.13), channel_id=1, source_target_pairs={{0,1},{1,2},{2,3},{3,4},{4,5},{5,6},{6,7},{8,9},{9,10},{10,11},{11... | collective-permute-start | bytes 3145736 | tf_op jit(solution)/shard_map/while/body/eval_jaxpr/ppermute | solution.py:27
  203.9 13.9 %collective-permute-start = (f32[32,64,128]{2,1,0:T(8,128)}, f32[32,64,128]{2,1,0:T(8,128)S(1)}, u32[]{:S(2)}, u32[]{:S(2)}) collective-permute-start(f32[32,64,128]{2,1,0:T(8,128)} %multiply_add_fusion.13), channel_id=1, source_target_pairs={{0,1},{1,2},{2,3},{3,4},{4,5},{5,6},{6,7},{8,9},{9,10},{10,11},{11... | collective-permute-start | bytes 3145736 | tf_op jit(solution)/shard_map/while/body/eval_jaxpr/ppermute | solution.py:27
  221.3 13.9 %collective-permute-start = (f32[32,64,128]{2,1,0:T(8,128)}, f32[32,64,128]{2,1,0:T(8,128)S(1)}, u32[]{:S(2)}, u32[]{:S(2)}) collective-permute-start(f32[32,64,128]{2,1,0:T(8,128)} %multiply_add_fusion.13), channel_id=1, source_target_pairs={{0,1},{1,2},{2,3},{3,4},{4,5},{5,6},{6,7},{8,9},{9,10},{10,11},{11... | collective-permute-start | bytes 3145736 | tf_op jit(solution)/shard_map/while/body/eval_jaxpr/ppermute | solution.py:27
  238.8 13.9 %collective-permute-start = (f32[32,64,128]{2,1,0:T(8,128)}, f32[32,64,128]{2,1,0:T(8,128)S(1)}, u32[]{:S(2)}, u32[]{:S(2)}) collective-permute-start(f32[32,64,128]{2,1,0:T(8,128)} %multiply_add_fusion.13), channel_id=1, source_target_pairs={{0,1},{1,2},{2,3},{3,4},{4,5},{5,6},{6,7},{8,9},{9,10},{10,11},{11... | collective-permute-start | bytes 3145736 | tf_op jit(solution)/shard_map/while/body/eval_jaxpr/ppermute | solution.py:27
  279.7 12.5 %all-gather.14.cloned.1.call-start = ((), (), s32[]{:S(2)}) async-start(), calls=%async_computation.5 | async-start | bytes 10321920 | tf_op jit(solution)/shard_map/all_gather | solution.py:274
  301.3 128.8 %while.16 = (s32[]{:T(128)}, f32[32,64,128]{2,1,0:T(8,128)S(1)}, f32[1,32]{1,0:T(1,128)S(1)}, f32[32,64,128]{2,1,0:T(8,128)}, s32[]{:T(128)}, /*index=5*/s32[]{:T(128)}) while((s32[]{:T(128)}, f32[32,64,128]{2,1,0:T(8,128)S(1)}, f32[1,32]{1,0:T(1,128)S(1)}, f32[32,64,128]{2,1,0:T(8,128)}, s32[]{:T(128)}, ...), condition=%wide.region_8.9_spmd.clone, body=%wide.region_7.8_spmd.clone.sunk | while | flops 1310723 | bytes 6291703 | solution.py:227
  304.9 14.3 %collective-permute-done.1 = bf16[32,64,128]{2,1,0:T(8,128)(2,1)} collective-permute-done((bf16[32,64,128]{2,1,0:T(8,128)(2,1)}, bf16[32,64,128]{2,1,0:T(8,128)(2,1)}, u32[]{:S(2)}, u32[]{:S(2)}) %collective-permute-start.1) | collective-permute-done | bytes 524320 | tf_op jit(solution)/shard_map/while/body/eval_jaxpr/ppermute | solution.py:27
  323.9 25.9 %collective-permute-done.1 = bf16[32,64,128]{2,1,0:T(8,128)(2,1)} collective-permute-done((bf16[32,64,128]{2,1,0:T(8,128)(2,1)}, bf16[32,64,128]{2,1,0:T(8,128)(2,1)}, u32[]{:S(2)}, u32[]{:S(2)}) %collective-permute-start.1) | collective-permute-done | bytes 524320 | tf_op jit(solution)/shard_map/while/body/eval_jaxpr/ppermute | solution.py:27
  354.5 10.5 %collective-permute-done.1 = bf16[32,64,128]{2,1,0:T(8,128)(2,1)} collective-permute-done((bf16[32,64,128]{2,1,0:T(8,128)(2,1)}, bf16[32,64,128]{2,1,0:T(8,128)(2,1)}, u32[]{:S(2)}, u32[]{:S(2)}) %collective-permute-start.1) | collective-permute-done | bytes 524320 | tf_op jit(solution)/shard_map/while/body/eval_jaxpr/ppermute | solution.py:27
  369.6 16.8 %collective-permute-done.1 = bf16[32,64,128]{2,1,0:T(8,128)(2,1)} collective-permute-done((bf16[32,64,128]{2,1,0:T(8,128)(2,1)}, bf16[32,64,128]{2,1,0:T(8,128)(2,1)}, u32[]{:S(2)}, u32[]{:S(2)}) %collective-permute-start.1) | collective-permute-done | bytes 524320 | tf_op jit(solution)/shard_map/while/body/eval_jaxpr/ppermute | solution.py:27
  391.1 9.5 %collective-permute-done.1 = bf16[32,64,128]{2,1,0:T(8,128)(2,1)} collective-permute-done((bf16[32,64,128]{2,1,0:T(8,128)(2,1)}, bf16[32,64,128]{2,1,0:T(8,128)(2,1)}, u32[]{:S(2)}, u32[]{:S(2)}) %collective-permute-start.1) | collective-permute-done | bytes 524320 | tf_op jit(solution)/shard_map/while/body/eval_jaxpr/ppermute | solution.py:27
  405.3 9.5 %collective-permute-done.1 = bf16[32,64,128]{2,1,0:T(8,128)(2,1)} collective-permute-done((bf16[32,64,128]{2,1,0:T(8,128)(2,1)}, bf16[32,64,128]{2,1,0:T(8,128)(2,1)}, u32[]{:S(2)}, u32[]{:S(2)}) %collective-permute-start.1) | collective-permute-done | bytes 524320 | tf_op jit(solution)/shard_map/while/body/eval_jaxpr/ppermute | solution.py:27
  419.5 9.5 %collective-permute-done.1 = bf16[32,64,128]{2,1,0:T(8,128)(2,1)} collective-permute-done((bf16[32,64,128]{2,1,0:T(8,128)(2,1)}, bf16[32,64,128]{2,1,0:T(8,128)(2,1)}, u32[]{:S(2)}, u32[]{:S(2)}) %collective-permute-start.1) | collective-permute-done | bytes 524320 | tf_op jit(solution)/shard_map/while/body/eval_jaxpr/ppermute | solution.py:27
  485.1 7.9 collective-permute-done.3
  495.2 7.2 multiply_reduce_fusion.14
  514.4 70.4 %all-gather.14.cloned.1.call-done = bf16[1024,4384]{1,0:T(8,128)(2,1)} async-done(((bf16[128,4384]{1,0:T(8,128)(2,1)}), bf16[1024,4384]{1,0:T(8,128)(2,1)}) %all-gather.14.cloned.1.call-update) | async-done | bytes 8978448 | tf_op jit(solution)/shard_map/all_gather | solution.py:274
  584.8 6.0 fusion.4
  597.5 124.4 %all-reduce.21.cloned.1.call-done = f32[470016]{0:T(1024)} async-done(((f32[470016]{0:T(1024)}), f32[470016]{0:T(1024)}) %all-reduce.21.cloned.1.call-update) | async-done | bytes 1880080
  726.1 24.1 %reduce-scatter.9.cloned.1.call-done = bf16[1,32,2048]{2,1,0:T(8,128)(2,1)} async-done(((bf16[4,32,2048]{2,1,0:T(8,128)(2,1)}), bf16[1,32,2048]{2,1,0:T(8,128)(2,1)}) %reduce-scatter.9.cloned.1.call-update) | async-done | bytes 131088
  752.1 29.5 %reduce-scatter.7.cloned.1.call-done = bf16[1,32,4384]{2,1,0:T(8,128)(2,1)} async-done(((bf16[4,32,4384]{2,1,0:T(8,128)(2,1)}), bf16[1,32,4384]{2,1,0:T(8,128)(2,1)}) %reduce-scatter.7.cloned.1.call-update) | async-done | bytes 280592
  (339 shorter events, 207.6 us)
Async XLA Ops:
  7.2 87.3 %all-gather.8.cloned.1.call-start = ((), (), s32[]{:S(2)}) async-start(), calls=%async_computation.2 | async-start | bytes 9461760 | tf_op jit(solution)/shard_map/all_gather | solution.py:158
  9.1 261.5 %all-gather.10.cloned.1.call-start = ((), (), s32[]{:S(2)}) async-start(), calls=%async_computation.3 | async-start | bytes 4325376 | tf_op jit(solution)/shard_map/all_gather | solution.py:159
  9.9 494.8 %all-gather.16.cloned.1.call-start = ((), (), s32[]{:S(2)}) async-start(), calls=%async_computation.6 | async-start | bytes 2359296 | tf_op jit(solution)/shard_map/all_gather | solution.py:275
  10.7 497.0 %all-gather.18.cloned.1.call-start = ((), (), s32[]{:S(2)}) async-start(), calls=%async_computation.7 | async-start | bytes 4718592 | tf_op jit(solution)/shard_map/all_gather | solution.py:276
  100.6 7.5 collective-permute-start.2
  122.4 20.4 %collective-permute-start = (f32[32,64,128]{2,1,0:T(8,128)}, f32[32,64,128]{2,1,0:T(8,128)S(1)}, u32[]{:S(2)}, u32[]{:S(2)}) collective-permute-start(f32[32,64,128]{2,1,0:T(8,128)} %multiply_add_fusion.13), channel_id=1, source_target_pairs={{0,1},{1,2},{2,3},{3,4},{4,5},{5,6},{6,7},{8,9},{9,10},{10,11},{11... | collective-permute-start | bytes 3145736 | tf_op jit(solution)/shard_map/while/body/eval_jaxpr/ppermute | solution.py:27
  144.0 24.3 %collective-permute-start = (f32[32,64,128]{2,1,0:T(8,128)}, f32[32,64,128]{2,1,0:T(8,128)S(1)}, u32[]{:S(2)}, u32[]{:S(2)}) collective-permute-start(f32[32,64,128]{2,1,0:T(8,128)} %multiply_add_fusion.13), channel_id=1, source_target_pairs={{0,1},{1,2},{2,3},{3,4},{4,5},{5,6},{6,7},{8,9},{9,10},{10,11},{11... | collective-permute-start | bytes 3145736 | tf_op jit(solution)/shard_map/while/body/eval_jaxpr/ppermute | solution.py:27
  169.5 33.2 %collective-permute-start = (f32[32,64,128]{2,1,0:T(8,128)}, f32[32,64,128]{2,1,0:T(8,128)S(1)}, u32[]{:S(2)}, u32[]{:S(2)}) collective-permute-start(f32[32,64,128]{2,1,0:T(8,128)} %multiply_add_fusion.13), channel_id=1, source_target_pairs={{0,1},{1,2},{2,3},{3,4},{4,5},{5,6},{6,7},{8,9},{9,10},{10,11},{11... | collective-permute-start | bytes 3145736 | tf_op jit(solution)/shard_map/while/body/eval_jaxpr/ppermute | solution.py:27
  203.9 16.3 %collective-permute-start = (f32[32,64,128]{2,1,0:T(8,128)}, f32[32,64,128]{2,1,0:T(8,128)S(1)}, u32[]{:S(2)}, u32[]{:S(2)}) collective-permute-start(f32[32,64,128]{2,1,0:T(8,128)} %multiply_add_fusion.13), channel_id=1, source_target_pairs={{0,1},{1,2},{2,3},{3,4},{4,5},{5,6},{6,7},{8,9},{9,10},{10,11},{11... | collective-permute-start | bytes 3145736 | tf_op jit(solution)/shard_map/while/body/eval_jaxpr/ppermute | solution.py:27
  221.3 16.3 %collective-permute-start = (f32[32,64,128]{2,1,0:T(8,128)}, f32[32,64,128]{2,1,0:T(8,128)S(1)}, u32[]{:S(2)}, u32[]{:S(2)}) collective-permute-start(f32[32,64,128]{2,1,0:T(8,128)} %multiply_add_fusion.13), channel_id=1, source_target_pairs={{0,1},{1,2},{2,3},{3,4},{4,5},{5,6},{6,7},{8,9},{9,10},{10,11},{11... | collective-permute-start | bytes 3145736 | tf_op jit(solution)/shard_map/while/body/eval_jaxpr/ppermute | solution.py:27
  238.8 16.3 %collective-permute-start = (f32[32,64,128]{2,1,0:T(8,128)}, f32[32,64,128]{2,1,0:T(8,128)S(1)}, u32[]{:S(2)}, u32[]{:S(2)}) collective-permute-start(f32[32,64,128]{2,1,0:T(8,128)} %multiply_add_fusion.13), channel_id=1, source_target_pairs={{0,1},{1,2},{2,3},{3,4},{4,5},{5,6},{6,7},{8,9},{9,10},{10,11},{11... | collective-permute-start | bytes 3145736 | tf_op jit(solution)/shard_map/while/body/eval_jaxpr/ppermute | solution.py:27
  279.1 232.4 %all-gather.12.cloned.1.call-start = ((), (), s32[]{:S(2)}) async-start(), calls=%async_computation.4 | async-start | bytes 2359296 | tf_op jit(solution)/shard_map/all_gather | solution.py:273
  279.7 305.1 %all-gather.14.cloned.1.call-start = ((), (), s32[]{:S(2)}) async-start(), calls=%async_computation.5 | async-start | bytes 10321920 | tf_op jit(solution)/shard_map/all_gather | solution.py:274
  303.6 15.6 %collective-permute-start.1 = (bf16[32,64,128]{2,1,0:T(8,128)(2,1)}, bf16[32,64,128]{2,1,0:T(8,128)(2,1)}, u32[]{:S(2)}, u32[]{:S(2)}) collective-permute-start(bf16[32,64,128]{2,1,0:T(8,128)(2,1)} %fusion.145), channel_id=1, source_target_pairs={{1,0},{2,1},{3,2},{4,3},{5,4},{6,5},{7,6},{9,8},{10,9},{11,10},{12... | collective-permute-start | bytes 1572872 | tf_op jit(solution)/shard_map/while/body/eval_jaxpr/ppermute | solution.py:27
  322.6 27.1 %collective-permute-start.1 = (bf16[32,64,128]{2,1,0:T(8,128)(2,1)}, bf16[32,64,128]{2,1,0:T(8,128)(2,1)}, u32[]{:S(2)}, u32[]{:S(2)}) collective-permute-start(bf16[32,64,128]{2,1,0:T(8,128)(2,1)} %fusion.145), channel_id=1, source_target_pairs={{1,0},{2,1},{3,2},{4,3},{5,4},{6,5},{7,6},{9,8},{10,9},{11,10},{12... | collective-permute-start | bytes 1572872 | tf_op jit(solution)/shard_map/while/body/eval_jaxpr/ppermute | solution.py:27
  353.2 11.8 %collective-permute-start.1 = (bf16[32,64,128]{2,1,0:T(8,128)(2,1)}, bf16[32,64,128]{2,1,0:T(8,128)(2,1)}, u32[]{:S(2)}, u32[]{:S(2)}) collective-permute-start(bf16[32,64,128]{2,1,0:T(8,128)(2,1)} %fusion.145), channel_id=1, source_target_pairs={{1,0},{2,1},{3,2},{4,3},{5,4},{6,5},{7,6},{9,8},{10,9},{11,10},{12... | collective-permute-start | bytes 1572872 | tf_op jit(solution)/shard_map/while/body/eval_jaxpr/ppermute | solution.py:27
  368.3 18.1 %collective-permute-start.1 = (bf16[32,64,128]{2,1,0:T(8,128)(2,1)}, bf16[32,64,128]{2,1,0:T(8,128)(2,1)}, u32[]{:S(2)}, u32[]{:S(2)}) collective-permute-start(bf16[32,64,128]{2,1,0:T(8,128)(2,1)} %fusion.145), channel_id=1, source_target_pairs={{1,0},{2,1},{3,2},{4,3},{5,4},{6,5},{7,6},{9,8},{10,9},{11,10},{12... | collective-permute-start | bytes 1572872 | tf_op jit(solution)/shard_map/while/body/eval_jaxpr/ppermute | solution.py:27
  389.8 10.8 %collective-permute-start.1 = (bf16[32,64,128]{2,1,0:T(8,128)(2,1)}, bf16[32,64,128]{2,1,0:T(8,128)(2,1)}, u32[]{:S(2)}, u32[]{:S(2)}) collective-permute-start(bf16[32,64,128]{2,1,0:T(8,128)(2,1)} %fusion.145), channel_id=1, source_target_pairs={{1,0},{2,1},{3,2},{4,3},{5,4},{6,5},{7,6},{9,8},{10,9},{11,10},{12... | collective-permute-start | bytes 1572872 | tf_op jit(solution)/shard_map/while/body/eval_jaxpr/ppermute | solution.py:27
  404.0 10.8 %collective-permute-start.1 = (bf16[32,64,128]{2,1,0:T(8,128)(2,1)}, bf16[32,64,128]{2,1,0:T(8,128)(2,1)}, u32[]{:S(2)}, u32[]{:S(2)}) collective-permute-start(bf16[32,64,128]{2,1,0:T(8,128)(2,1)} %fusion.145), channel_id=1, source_target_pairs={{1,0},{2,1},{3,2},{4,3},{5,4},{6,5},{7,6},{9,8},{10,9},{11,10},{12... | collective-permute-start | bytes 1572872 | tf_op jit(solution)/shard_map/while/body/eval_jaxpr/ppermute | solution.py:27
  418.2 10.8 %collective-permute-start.1 = (bf16[32,64,128]{2,1,0:T(8,128)(2,1)}, bf16[32,64,128]{2,1,0:T(8,128)(2,1)}, u32[]{:S(2)}, u32[]{:S(2)}) collective-permute-start(bf16[32,64,128]{2,1,0:T(8,128)(2,1)} %fusion.145), channel_id=1, source_target_pairs={{1,0},{2,1},{3,2},{4,3},{5,4},{6,5},{7,6},{9,8},{10,9},{11,10},{12... | collective-permute-start | bytes 1572872 | tf_op jit(solution)/shard_map/while/body/eval_jaxpr/ppermute | solution.py:27
  483.2 9.8 %collective-permute-start.3 = (f32[3,2304]{1,0:T(4,128)S(1)}, f32[3,2304]{1,0:T(4,128)S(1)}, u32[]{:S(2)}, u32[]{:S(2)}) collective-permute-start(f32[3,2304]{1,0:T(4,128)S(1)} %pad_add_fusion.1), channel_id=1, source_target_pairs={{1,0},{2,1},{3,2},{4,3},{5,4},{6,5},{7,6},{9,8},{10,9},{11,10},{12... | collective-permute-start | bytes 82952 | tf_op jit(solution)/shard_map/ppermute | solution.py:27
  494.2 227.7 %all-reduce.21.cloned.1.call-start = ((), (), s32[]{:S(2)}) async-start(), calls=%async_computation.8 | async-start | bytes 3760128
  504.6 245.5 %reduce-scatter.9.cloned.1.call-start = ((), (), s32[]{:S(2)}) async-start(), calls=%async_computation.10 | async-start | bytes 655360
  511.4 270.2 %reduce-scatter.7.cloned.1.call-start = ((), (), s32[]{:S(2)}) async-start(), calls=%async_computation.9 | async-start | bytes 1433600
  (85 other events, 1738.9 us)
Sparse Core Ops, SparseCore 0:
  11.4 83.0 all-gather.7
  98.1 60.4 all-gather.9
  160.8 33.7 all-gather.15
  279.3 63.3 all-gather.17
  344.7 33.5 all-gather.11
  494.3 90.4 all-gather.13
  590.2 131.6 all-reduce.20
  725.3 24.8 reduce-scatter.8
  753.1 28.4 reduce-scatter.6
